TPU v7x, 32 devices: a whole 2x2x4 slice. The times are simulated.
32 devices in a mesh: fsdp: 8 (over y, x, core), tp: 4 (over z).
Axes of the slice: x: 2, y: 2, z: 4, core: 2. Of those that a mesh axis runs over, the one named last changes fastest.
Arguments:
- residual: bfloat16 [4096, 2048], P(('fsdp', 'tp')), may hold values from -6 to 6
- norm_gain: bfloat16 [2048], P(('fsdp', 'tp')), may hold values from 0.099609375 to 1.8984375
- norm_shift: bfloat16 [2048], P(('fsdp', 'tp')), may hold values from -1.75 to 1.75
- qkv_weight: bfloat16 [3, 2048, 2048], P(None, 'fsdp', 'tp'), may hold values from -0.125 to 0.125
- qkv_bias: bfloat16 [3, 2048], P(None, ('tp', 'fsdp')), may hold values from -1.75 to 1.75
- dense_weight: bfloat16 [2048, 2048], P('tp', 'fsdp'), may hold values from -0.75 to 0.75
- dense_bias: bfloat16 [2048], P(('fsdp', 'tp')), may hold values from -1.75 to 1.75
- inner_weight: bfloat16 [2048, 8192], P('fsdp', 'tp'), may hold values from -0.125 to 0.125
- inner_bias: bfloat16 [8192], P(('tp', 'fsdp')), may hold values from -1.75 to 1.75
- outer_weight: bfloat16 [8192, 2048], P('tp', 'fsdp'), may hold values from -0.0625 to 0.0625
- outer_bias: bfloat16 [2048], P(('fsdp', 'tp')), may hold values from -1.75 to 1.75
- cotangent: bfloat16 [4096, 2048], P(('fsdp', 'tp')), may hold values from -6 to 6
- segment: int32 [4096], replicated, may hold values from 0 to 38, as said below
- ancestors: int32 [39, 3], replicated, may hold values from 0 to 38, as said below
- valid_slot: int32 [4096], replicated, may hold values from 0 to 1, as said below
Outputs:
- output: bfloat16 [4096, 2048], P(('fsdp', 'tp'))
- residual_grad: bfloat16 [4096, 2048], P(('fsdp', 'tp'))
- norm_gain_grad: float32 [2048], P(('fsdp', 'tp'))
- norm_shift_grad: float32 [2048], P(('fsdp', 'tp'))
- qkv_weight_grad: float32 [3, 2048, 2048], P(None, 'fsdp', 'tp')
- qkv_bias_grad: float32 [3, 2048], P(None, ('tp', 'fsdp'))
- dense_weight_grad: float32 [2048, 2048], P('tp', 'fsdp')
- dense_bias_grad: float32 [2048], P(('fsdp', 'tp'))
- inner_weight_grad: float32 [2048, 8192], P('fsdp', 'tp')
- inner_bias_grad: float32 [8192], P(('tp', 'fsdp'))
- outer_weight_grad: float32 [8192, 2048], P('tp', 'fsdp')
- outer_bias_grad: float32 [2048], P(('fsdp', 'tp'))
Inputs may be any that keep to these rules, and one draw needn't show every extreme that they name: Each of the 3 trees fills 1024 consecutive slots, in order of slots: a trunk of 640 slots, then four branches and eight leaves of 32 slots each, two leaves to a branch, each leaf after its branch; the slots of a segment are consecutive and carry its id; padding slots carry 0. `ancestors`: row s names the trunk, branch and leaf segment of the path that ends in segment s, repeating s where the path is shorter; each tree's segments name only that tree's segments. `valid_slot`: 1 on exactly the slots that trees fill, 0 on the other 1024 slots.
All inputs are finite; a program needn't handle non-finite values.
Results may differ from a plain program's by a relative error of at most 0.0098.
Values may be sent and summed in bfloat16 or wider, within the bound.
No kernel may reach another device: no remote copies, remote signals or barrier semaphores. Data moves between devices by JAX's collectives and lax.ppermute only.
A program may use at most 192 MiB of HBM per device.

v0:
```python
import jax
import jax.numpy as jnp
from jax import lax
from jax.sharding import PartitionSpec as P

HEAD_DIM = 64
ROTARY = 32
TREE_LEN = 1024
EPSILON = 1e-05


def passed_along(value, axis, steps):
    count = lax.axis_size(axis)
    initial, last = (max(0, -steps), min(count, count - steps))
    return lax.ppermute(value, axis, [(source, source + steps) for source in range(initial, last)])


def norm_rows(inputs_f, gain_f, shift_f):
    row_mean = jnp.mean(inputs_f, axis=-1, keepdims=True)
    centered = inputs_f - row_mean
    variance = jnp.mean(centered * centered, axis=-1, keepdims=True)
    return centered * lax.rsqrt(variance + EPSILON) * gain_f + shift_f


def tree_allowed(query_seg, query_slot, query_valid, key_seg, key_slot, key_valid, ancestors):
    seg_ids = jnp.arange(ancestors.shape[0], dtype=jnp.int32)
    onehot = (query_seg[:, None] == seg_ids[None, :]).astype(jnp.int32)
    path_ids = jnp.sum(onehot[:, :, None] * ancestors[None, :, :], axis=1)
    linked = (
        (key_seg[None, :] == path_ids[:, 0:1])
        | (key_seg[None, :] == path_ids[:, 1:2])
        | (key_seg[None, :] == path_ids[:, 2:3])
    )
    earlier = key_slot[None, :] <= query_slot[:, None]
    usable = (key_valid[None, :] == 1) & (query_valid[:, None] == 1)
    return linked & earlier & usable | (key_slot[None, :] == query_slot[:, None])


def rotate(tensor, positions, direction):
    half_rot = ROTARY // 2
    freq = 10000.0 ** (-(jnp.arange(half_rot, dtype=jnp.float32) * 2.0 / ROTARY))
    angle = direction * positions.astype(jnp.float32)[:, None] * freq[None, :]
    cosine = jnp.cos(angle)[:, None, :]
    sine = jnp.sin(angle)[:, None, :]
    first = tensor[..., :half_rot]
    second = tensor[..., half_rot:ROTARY]
    return jnp.concatenate(
        [first * cosine - second * sine, second * cosine + first * sine, tensor[..., ROTARY:]],
        axis=-1,
    )


def body(
    residual,
    norm_gain,
    norm_shift,
    qkv_weight,
    qkv_bias,
    dense_weight,
    dense_bias,
    inner_weight,
    inner_bias,
    outer_weight,
    outer_bias,
    cotangent,
    segment,
    ancestors,
    valid_slot,
):
    f32 = jnp.float32
    bf16 = jnp.bfloat16
    tp_size = lax.axis_size("tp")
    local_rows = residual.shape[0]
    group_rows = local_rows * tp_size
    head_cols = qkv_weight.shape[2]
    head_count = head_cols // HEAD_DIM
    reach_back = (TREE_LEN - 2) // group_rows + 1
    front_rows = reach_back * group_rows
    window = front_rows + group_rows
    block_rows = min(512, group_rows)
    block_count = group_rows // block_rows
    scaling = HEAD_DIM ** (-0.5)
    base_slot = lax.axis_index("fsdp") * group_rows
    vectors = (
        lax.all_gather(norm_gain, ("fsdp", "tp"), axis=0, tiled=True),
        lax.all_gather(norm_shift, ("fsdp", "tp"), axis=0, tiled=True),
        lax.all_gather(dense_bias, ("fsdp", "tp"), axis=0, tiled=True),
        lax.all_gather(outer_bias, ("fsdp", "tp"), axis=0, tiled=True),
    )
    gain_f = vectors[0].astype(f32)
    shift_f = vectors[1].astype(f32)
    bias_sum = vectors[2].astype(f32) + vectors[3].astype(f32)
    seg_front = jnp.concatenate([jnp.zeros((front_rows,), jnp.int32), segment])
    valid_front = jnp.concatenate([jnp.zeros((front_rows,), jnp.int32), valid_slot])
    query_slot = base_slot + jnp.arange(group_rows, dtype=jnp.int32)
    query_seg = lax.dynamic_slice_in_dim(segment, base_slot, group_rows)
    query_valid = lax.dynamic_slice_in_dim(valid_slot, base_slot, group_rows)
    key_slot = base_slot - front_rows + jnp.arange(window, dtype=jnp.int32)
    key_seg = lax.dynamic_slice_in_dim(seg_front, base_slot, window)
    key_valid = lax.dynamic_slice_in_dim(valid_front, base_slot, window)

    def allowed_for():
        return tree_allowed(
            query_seg, query_slot, query_valid, key_seg, key_slot, key_valid, ancestors
        )

    def count_keys(block_num):
        return jnp.sum(allowed_for().astype(jnp.int32), axis=1) - 1

    block_ids = jnp.arange(block_count, dtype=jnp.int32)
    positions = lax.map(count_keys, block_ids).reshape(group_rows)
    inputs_f = residual.astype(f32)
    normed_local = norm_rows(inputs_f, gain_f, shift_f).astype(bf16)

    def key_window(keys_own, values_own):
        key_parts = []
        value_parts = []
        for distance in range(reach_back, 0, -1):
            got_keys, got_values = passed_along((keys_own, values_own), "fsdp", distance)
            key_parts.append(got_keys)
            value_parts.append(got_values)
        return (
            jnp.concatenate(key_parts + [keys_own], axis=0),
            jnp.concatenate(value_parts + [values_own], axis=0),
        )

    def forward_pieces():
        gathered = (
            lax.all_gather(qkv_weight, "fsdp", axis=1, tiled=True),
            lax.all_gather(qkv_bias, "fsdp", axis=1, tiled=True),
            lax.all_gather(dense_weight, "fsdp", axis=1, tiled=True),
            lax.all_gather(inner_weight, "fsdp", axis=0, tiled=True),
            lax.all_gather(inner_bias, "fsdp", axis=0, tiled=True),
            lax.all_gather(outer_weight, "fsdp", axis=1, tiled=True),
        )
        normed = lax.all_gather(normed_local, "tp", axis=0, tiled=True)
        w_qkv = gathered[0]
        mixed = (
            jnp.einsum("td,sde->ste", normed, w_qkv, preferred_element_type=f32)
            + gathered[1].astype(f32)[:, None, :]
        )
        queries = rotate(mixed[0].reshape(group_rows, head_count, HEAD_DIM), positions, 1.0).astype(
            bf16
        )
        keys_own = (
            rotate(mixed[1].reshape(group_rows, head_count, HEAD_DIM), positions, 1.0)
            .astype(bf16)
            .reshape(group_rows, head_cols)
        )
        values_own = mixed[2].astype(bf16)
        keys_win, values_win = key_window(keys_own, values_own)
        keys_win = keys_win.reshape(window, head_count, HEAD_DIM)
        values_win = values_win.reshape(window, head_count, HEAD_DIM)

        def attend(block_num):
            scores = (
                jnp.einsum("qhe,khe->hqk", queries, keys_win, preferred_element_type=f32) * scaling
            )
            scores = jnp.where(allowed_for()[None], scores, -jnp.inf)
            top_score = jnp.max(scores, axis=-1, keepdims=True)
            expo = jnp.exp(scores - top_score)
            summed = jnp.sum(expo, axis=-1, keepdims=True)
            probs_low = (expo / summed).astype(bf16)
            attended = jnp.einsum("hqk,khe->qhe", probs_low, values_win, preferred_element_type=f32)
            return (attended, (top_score + jnp.log(summed))[..., 0])

        attended, log_sums = lax.map(attend, block_ids)
        attended = attended.reshape(group_rows, head_cols).astype(bf16)
        pre_act = jnp.dot(normed, gathered[3], preferred_element_type=f32) + gathered[4].astype(f32)
        activated = jax.nn.gelu(pre_act, approximate=True).astype(bf16)
        return (
            gathered,
            normed,
            queries,
            keys_win,
            values_win,
            attended,
            log_sums,
            pre_act,
            activated,
        )

    gathered, normed, queries, keys_win, values_win, attended, log_sums, pre_act, activated = (
        forward_pieces()
    )
    partial_rows = jnp.dot(attended, gathered[2], preferred_element_type=f32) + jnp.dot(
        activated, gathered[5], preferred_element_type=f32
    )
    summed_rows = lax.psum_scatter(partial_rows, "tp", scatter_dimension=0, tiled=True)
    output = (inputs_f + summed_rows + bias_sum).astype(bf16)
    out_bias_grad = jnp.sum(cotangent.astype(f32), axis=0)
    grad_rows = lax.all_gather(cotangent, "tp", axis=0, tiled=True)
    gathered, normed, queries, keys_win, values_win, attended, log_sums, pre_act, activated = (
        forward_pieces()
    )
    w_qkv = gathered[0]
    w_dense = gathered[2]
    w_inner = gathered[3]
    w_outer = gathered[5]
    outer_grad = jnp.einsum("tf,td->fd", activated, grad_rows, preferred_element_type=f32)
    act_grad = jnp.einsum("td,fd->tf", grad_rows, w_outer, preferred_element_type=f32)
    unused_value, gelu_pull = jax.vjp(
        lambda inputs_g: jax.nn.gelu(inputs_g, approximate=True), pre_act
    )
    pre_grad = gelu_pull(act_grad)[0].astype(bf16)
    inner_grad = jnp.einsum("td,tf->df", normed, pre_grad, preferred_element_type=f32)
    inner_bias_grad = jnp.sum(pre_grad.astype(f32), axis=0)
    normed_grad = jnp.einsum("tf,df->td", pre_grad, w_inner, preferred_element_type=f32)
    dense_grad = jnp.einsum("tc,td->cd", attended, grad_rows, preferred_element_type=f32)
    attn_grad = (
        jnp.einsum("td,cd->tc", grad_rows, w_dense, preferred_element_type=f32)
        .astype(bf16)
        .reshape(group_rows, head_count, HEAD_DIM)
    )

    def attend_back(carry, inputs_b):
        key_acc, value_acc = carry
        block_num, log_block = inputs_b
        scores = jnp.einsum("qhe,khe->hqk", queries, keys_win, preferred_element_type=f32) * scaling
        probs = jnp.where(allowed_for()[None], jnp.exp(scores - log_block[..., None]), 0.0)
        probs_low = probs.astype(bf16)
        prob_grad = jnp.einsum("qhe,khe->hqk", attn_grad, values_win, preferred_element_type=f32)
        row_dot = jnp.sum(probs * prob_grad, axis=-1, keepdims=True)
        score_grad = (probs * (prob_grad - row_dot)).astype(bf16)
        query_grad = (
            jnp.einsum("hqk,khe->qhe", score_grad, keys_win, preferred_element_type=f32) * scaling
        )
        key_part = (
            key_acc
            + jnp.einsum("hqk,qhe->khe", score_grad, queries, preferred_element_type=f32) * scaling
        )
        value_part = value_acc + jnp.einsum(
            "hqk,qhe->khe", probs_low, attn_grad, preferred_element_type=f32
        )
        key_acc = key_part
        value_acc = value_part
        return ((key_acc, value_acc), query_grad)

    zero_window = jnp.zeros((window, head_count, HEAD_DIM), f32)
    (key_acc, value_acc), query_grads = lax.scan(
        attend_back, (zero_window, zero_window), (block_ids, log_sums)
    )
    key_flat = key_acc.reshape(window, head_cols)
    value_flat = value_acc.reshape(window, head_cols)
    own_key = key_flat[front_rows:]
    own_value = value_flat[front_rows:]
    for distance in range(1, reach_back + 1):
        lower = front_rows - distance * group_rows
        got_key, got_value = passed_along(
            (key_flat[lower : lower + group_rows], value_flat[lower : lower + group_rows]),
            "fsdp",
            -distance,
        )
        own_key = own_key + got_key
        own_value = own_value + got_value
    query_pre = rotate(
        query_grads.reshape(group_rows, head_count, HEAD_DIM), positions, -1.0
    ).reshape(group_rows, head_cols)
    key_pre = rotate(own_key.reshape(group_rows, head_count, HEAD_DIM), positions, -1.0).reshape(
        group_rows, head_cols
    )
    qkv_grad = jnp.stack([query_pre, key_pre, own_value]).astype(bf16)
    qkv_weight_part = jnp.einsum("td,ste->sde", normed, qkv_grad, preferred_element_type=f32)
    qkv_bias_part = jnp.sum(qkv_grad.astype(f32), axis=1)
    normed_grad = normed_grad + jnp.einsum(
        "ste,sde->td", qkv_grad, w_qkv, preferred_element_type=f32
    )
    local_grad = lax.psum_scatter(normed_grad, "tp", scatter_dimension=0, tiled=True)
    unused_norm, norm_pull = jax.vjp(norm_rows, inputs_f, gain_f, shift_f)
    input_grad, gain_grad, shift_grad = norm_pull(local_grad)
    residual_grad = (cotangent.astype(f32) + input_grad).astype(bf16)
    weight_sums = (
        lax.psum_scatter(qkv_weight_part, "fsdp", scatter_dimension=1, tiled=True),
        lax.psum_scatter(qkv_bias_part, "fsdp", scatter_dimension=1, tiled=True),
        lax.psum_scatter(dense_grad, "fsdp", scatter_dimension=1, tiled=True),
        lax.psum_scatter(inner_grad, "fsdp", scatter_dimension=0, tiled=True),
        lax.psum_scatter(inner_bias_grad, "fsdp", scatter_dimension=0, tiled=True),
        lax.psum_scatter(outer_grad, "fsdp", scatter_dimension=1, tiled=True),
    )
    vector_sums = (
        lax.psum_scatter(gain_grad, ("fsdp", "tp"), scatter_dimension=0, tiled=True),
        lax.psum_scatter(shift_grad, ("fsdp", "tp"), scatter_dimension=0, tiled=True),
        lax.psum_scatter(out_bias_grad, ("fsdp", "tp"), scatter_dimension=0, tiled=True),
    )
    return (
        output,
        residual_grad,
        vector_sums[0],
        vector_sums[1],
        weight_sums[0],
        weight_sums[1],
        weight_sums[2],
        vector_sums[2],
        weight_sums[3],
        weight_sums[4],
        weight_sums[5],
        vector_sums[2],
    )


def solution(mesh):
    return jax.shard_map(
        body,
        mesh=mesh,
        in_specs=(
            P(("fsdp", "tp"), None),
            P(("fsdp", "tp")),
            P(("fsdp", "tp")),
            P(None, "fsdp", "tp"),
            P(None, ("tp", "fsdp")),
            P("tp", "fsdp"),
            P(("fsdp", "tp")),
            P("fsdp", "tp"),
            P(("tp", "fsdp")),
            P("tp", "fsdp"),
            P(("fsdp", "tp")),
            P(("fsdp", "tp"), None),
            P(),
            P(),
            P(),
        ),
        out_specs=(
            P(("fsdp", "tp"), None),
            P(("fsdp", "tp"), None),
            P(("fsdp", "tp")),
            P(("fsdp", "tp")),
            P(None, "fsdp", "tp"),
            P(None, ("tp", "fsdp")),
            P("tp", "fsdp"),
            P(("fsdp", "tp")),
            P("fsdp", "tp"),
            P(("tp", "fsdp")),
            P("tp", "fsdp"),
            P(("fsdp", "tp")),
        ),
        check_vma=False,
    )
```

profile of v0, /device:TPU:0, one launch (start us, length us, event | category | flops | bytes accessed | tf_op | source)
XLA Modules:
  0.0 1016.9 jit_solution(10757736382496534110)
XLA Ops:
  10.7 42.2 %all-reduce.11 = (bf16[2048]{0:T(1024)(128)(2,1)S(1)}, bf16[2048]{0:T(1024)(128)(2,1)S(1)}, bf16[2048]{0:T(1024)(128)(2,1)}, bf16[2048]{0:T(1024)(128)(2,1)}) all-reduce(bf16[2048]{0:T(1024)(128)(2,1)S(1)} %dynamic-update-slice.1, bf16[2048]{0:T(1024)(128)(2,1)S(1)} %dynamic-update-slice, ...), channel_id=1, replica_groups=mesh['fsdp'=8,'tp'=4] {'fsdp','tp'}, use_global_device_ids=true, to_apply=%add.3 | all-reduce | flops 8192 | bytes 32768
  56.0 2.2 fusion.31
  58.3 2.3 copy.69
  63.7 1.9 convert_reduce_fusion.2
  65.6 10.2 %all-gather = bf16[8,64,3]{1,2,0:T(4,128)(2,1)S(1)} all-gather(bf16[1,64,3]{1,2,0:T(4,128)(2,1)S(1)} %bitcast.110), channel_id=1, replica_groups=mesh['fsdp'=8,'tp'=4] {'fsdp'}, dimensions={0}, use_global_device_ids=true | all-gather | bytes 3456 | tf_op jit(solution)/shard_map/all_gather | solution.py:130
  75.9 7.9 all-gather.1
  85.4 19.4 %all-gather.9.cloned.1.call-done = bf16[512,2048]{1,0:T(8,128)(2,1)} async-done(((bf16[128,2048]{1,0:T(8,128)(2,1)}), bf16[512,2048]{1,0:T(8,128)(2,1)}) %all-gather.9.cloned.1.call-update) | async-done | bytes 2097168 | tf_op jit(solution)/shard_map/all_gather | solution.py:136
  104.8 47.9 %all-gather.11.cloned.1.call-done = bf16[3,2048,512]{1,2,0:T(8,128)(2,1)} async-done(((bf16[3,256,512]{1,2,0:T(8,128)(2,1)}), bf16[3,2048,512]{1,2,0:T(8,128)(2,1)}) %all-gather.11.cloned.1.call-update) | async-done | bytes 6291472 | tf_op jit(solution)/shard_map/all_gather | solution.py:129
  152.6 6.2 add_bitcast_fusion
  160.6 4.2 collective-permute-start.2
  164.7 2.7 collective-permute-start.3
  167.4 32.8 %all-gather.19.cloned.1.call-done = bf16[512,2048]{1,0:T(8,128)(2,1)} async-done(((bf16[128,2048]{1,0:T(8,128)(2,1)}), bf16[512,2048]{1,0:T(8,128)(2,1)}) %all-gather.19.cloned.1.call-update) | async-done | bytes 2097168 | tf_op jit(solution)/shard_map/all_gather | solution.py:192
  200.2 28.7 %all-gather.13.cloned.1.call-done = bf16[512,2048]{1,0:T(8,128)(2,1)} async-done(((bf16[512,256]{1,0:T(8,128)(2,1)}), bf16[512,2048]{1,0:T(8,128)(2,1)}) %all-gather.13.cloned.1.call-update) | async-done | bytes 2097168 | tf_op jit(solution)/shard_map/all_gather | solution.py:131
  228.9 3.5 convolution_convert_fusion
  233.8 3.4 collective-permute-start
  237.2 2.2 collective-permute-start.1
  239.4 11.9 %select_reduce_fusion = (f32[8,512]{1,0:T(8,128)S(1)}, f32[8,512,1536]{2,1,0:T(8,128)}) fusion(pred[512,1536]{1,0:T(8,128)(4,1)S(1)} %get-tuple-element.236, bf16[512,8,64]{0,2,1:T(8,128)(2,1)S(1)} %maximum_convert_fusion, bf16[512,8,64]{0,2,1:T(8,128)(2,1)} %bitcast.14, bf16[512,8,64]{0,2,1:T(8,128)(2,1)} %bitcast.13, bf16[512,8,32]{0,2,1:T(8,128)(2,1)S(1)} %slice.202, ...), kind=kOutput, calls=%fused_computation.5 | convolution fusion | flops 830468096 | bytes 28065792 | tf_op jit(solution)/shard_map/while/body/eval_jaxpr/qhe,khe->hqk/dot_general | solution.py:157
  251.3 11.6 %fusion = f32[8,512]{1,0:T(8,128)S(1)} fusion(f32[8,512,1536]{2,1,0:T(8,128)} %get-tuple-element.268, f32[8,512]{1,0:T(8,128)S(1)} %get-tuple-element.267, pred[512,1536]{1,0:T(8,128)(4,1)S(1)} %get-tuple-element.236), kind=kLoop, calls=%fused_computation.6 | loop fusion | flops 25161728 | bytes 25985024 | tf_op jit(solution)/shard_map/while/body/eval_jaxpr/reduce_sum | solution.py:162
  263.5 19.6 %multiply_reduce_fusion = (f32[8,512]{1,0:T(8,128)S(1)}, f32[8,512,1536]{2,1,0:T(8,128)}) fusion(f32[8,512,1536]{2,1,0:T(8,128)} %get-tuple-element.268, f32[8,512]{1,0:T(8,128)S(1)} %log_add_fusion, pred[512,1536]{1,0:T(8,128)(4,1)S(1)} %get-tuple-element.236, bf16[512,8,64]{0,2,1:T(8,128)(2,1)S(1)} %bitcast.100, bf16[1536,8,64]{0,2,1:T(8,128)(2,1)S(1)} %bitcast.82), kind=kOutput, calls=%fused_computation.1 | convolution fusion | flops 836759552 | bytes 53248000 | tf_op jit(solution)/shard_map/while/body/eval_jaxpr/qhe,khe->hqk/dot_general | solution.py:222
  283.1 17.4 %multiply_convert_fusion = bf16[8,512,1536]{2,1,0:T(8,128)(2,1)S(1)} fusion(f32[8,512,1536]{2,1,0:T(8,128)} %get-tuple-element.270, f32[8,512,1536]{2,1,0:T(8,128)} %get-tuple-element.268, f32[8,512]{1,0:T(8,128)S(1)} %get-tuple-element.269, f32[8,512]{1,0:T(8,128)S(1)} %log_add_fusion, pred[512,1536]{1,0:T(8,128)(4,1)S(1)} %get-tuple-element.236), kind=kLoop, calls=%fused_computation | loop fusion | flops 37748736 | bytes 63733760 | tf_op jit(solution)/shard_map/while/body/eval_jaxpr/convert_element_type | solution.py:224
  300.5 2.3 fusion.13
  302.8 2.7 copy-done
  305.4 1.8 fusion.57
  309.8 10.9 %fusion.14 = f32[1536,8,64]{0,2,1:T(8,128)S(1)} fusion(bf16[512,8,64]{0,2,1:T(8,128)(2,1)S(1)} %bitcast.101, f32[8,512,1536]{2,1,0:T(8,128)} %get-tuple-element.268, f32[8,512]{1,0:T(8,128)S(1)} %log_add_fusion, pred[512,1536]{1,0:T(8,128)(4,1)S(1)} %get-tuple-element.236), kind=kOutput, calls=%fused_computation.26 | convolution fusion | flops 830472192 | bytes 29638656 | tf_op jit(solution)/shard_map/while/body/eval_jaxpr/hqk,qhe->khe/dot_general | solution.py:232
  320.7 1.6 fusion.58
  322.3 2.5 copy.71
  328.8 9.0 fusion.26
  338.8 1.6 copy.72
  340.4 22.6 %collective-permute-done.5 = f32[512,512]{0,1:T(8,128)} collective-permute-done((f32[512,512]{0,1:T(8,128)}, f32[512,512]{0,1:T(8,128)}, u32[]{:S(2)}, u32[]{:S(2)}) %collective-permute-start.5) | collective-permute-done | bytes 1048608 | tf_op jit(solution)/shard_map/ppermute | solution.py:15
  363.0 2.2 fusion.38
  366.0 1.6 subtract_convert_fusion.1
  368.4 2.0 copy.74
  370.4 1.8 pad_maximum_fusion.7
  372.2 2.0 copy.75
  374.3 11.8 %collective-permute-done.7 = f32[512,512]{1,0:T(8,128)} collective-permute-done((f32[512,512]{1,0:T(8,128)}, f32[512,512]{1,0:T(8,128)}, u32[]{:S(2)}, u32[]{:S(2)}) %collective-permute-start.7) | collective-permute-done | bytes 1048608 | tf_op jit(solution)/shard_map/ppermute | solution.py:15
  386.1 1.8 fusion.40
  388.7 1.4 convert_reduce_fusion.1
  391.0 8.8 reduce-scatter.12.cloned.1.call-start
  399.8 10.5 %fusion.61 = f32[512,2048]{1,0:T(8,128)} fusion(bf16[512,2048]{1,0:T(8,128)(2,1)} %all-gather.9.cloned.1.call-done, bf16[2048,2048]{1,0:T(8,128)(2,1)} %all-gather.15.cloned.1.call-done), kind=kOutput, calls=%fused_computation.123 | convolution fusion | flops 4294967296 | bytes 14680064 | tf_op jit(solution)/shard_map/dot_general | solution.py:169
  410.4 9.8 all-gather.17.cloned.1.call-done
  420.2 12.2 %convert_reduce_fusion = (f32[2048]{0:T(1024)S(1)}, bf16[512,2048]{1,0:T(8,128)(2,1)S(1)}) fusion(f32[512,2048]{1,0:T(8,128)} %fusion.61, f32[2048]{0:T(1024)S(1)} %bitcast.106, bf16[512,2048]{1,0:T(8,128)(2,1)} %all-gather.19.cloned.1.call-done, bf16[2048,2048]{1,0:T(8,128)(2,1)} %all-gather.17.cloned.1.call-done), kind=kOutput, calls=%fused_computation.22 | convolution fusion | flops 4319082496 | bytes 16793600 | tf_op jit(solution)/shard_map/td,fd->tf/dot_general | solution.py:201
  432.5 4.8 fusion.62
  437.3 7.9 bitcast_add_fusion
  446.0 11.6 %fusion.27 = bf16[8,64,512]{2,1,0:T(8,128)(2,1)S(1)} fusion(bf16[1536,8,64]{0,2,1:T(8,128)(2,1)S(1)} %bitcast.83, f32[8,512,1536]{2,1,0:T(8,128)} %get-tuple-element.268, f32[8,512]{1,0:T(8,128)S(1)} %copy-done.19, f32[8,512]{1,0:T(8,128)S(1)} %get-tuple-element.267, pred[512,1536]{1,0:T(8,128)(4,1)S(1)} %get-tuple-element.236), kind=kOutput, calls=%fused_computation.51 | convolution fusion | flops 837025792 | bytes 28082176 | tf_op jit(solution)/shard_map/while/body/eval_jaxpr/hqk,khe->qhe/dot_general | solution.py:164
  457.6 8.1 fusion.54
  465.7 3.4 convolution_add_fusion
  470.3 8.0 convolution_bitcast_fusion
  478.4 1.5 copy-done.11
  479.9 3.3 fusion.63
  483.5 12.6 %fusion.64 = f32[2048,2048]{1,0:T(8,128)} fusion(bf16[512,2048]{1,0:T(8,128)(2,1)} %all-gather.9.cloned.1.call-done, bf16[512,2048]{1,0:T(8,128)(2,1)} %copy-done.37), kind=kOutput, calls=%fused_computation.126 | convolution fusion | flops 4294967296 | bytes 20971520 | tf_op jit(solution)/shard_map/td,tf->df/dot_general | solution.py:206
  496.1 11.9 %fusion.53 = f32[2048,2048]{1,0:T(8,128)} fusion(bf16[512,2048]{1,0:T(8,128)(2,1)S(1)} %copy-done.11, f32[512,2048]{1,0:T(8,128)} %fusion.61, f32[2048]{0:T(1024)S(1)} %bitcast.108), kind=kOutput, calls=%fused_computation.116 | convolution fusion | flops 4305453056 | bytes 23076864 | tf_op jit(solution)/shard_map/tf,td->fd/dot_general | solution.py:200
  509.9 1.4 copy.82
  511.4 14.1 %all-reduce.9 = f32[2048]{0:T(1024)S(1)} all-reduce(f32[2048]{0:T(1024)S(1)} %get-tuple-element.233), channel_id=11, replica_groups=mesh['fsdp'=8,'tp'=4] {'fsdp'}, use_global_device_ids=true, to_apply=%region_23.24.clone | all-reduce | flops 2048 | bytes 16384
  526.1 10.6 %reduce-scatter.12.cloned.1.call-done = f32[128,2048]{1,0:T(8,128)} async-done(((f32[512,2048]{1,0:T(8,128)}), f32[128,2048]{1,0:T(8,128)}) %reduce-scatter.12.cloned.1.call-update) | async-done | bytes 1048592 | tf_op jit(solution)/shard_map/reduce_scatter | solution.py:268
  536.7 1.6 fusion.55
  538.3 1.7 fusion.32
  540.0 76.3 %reduce-scatter.10.cloned.1.call-done = f32[128,2048]{1,0:T(8,128)} async-done(((f32[512,2048]{1,0:T(8,128)}), f32[128,2048]{1,0:T(8,128)}) %reduce-scatter.10.cloned.1.call-update) | async-done | bytes 1048592 | tf_op jit(solution)/shard_map/reduce_scatter | solution.py:189
  616.3 3.2 convert_reduce_fusion.4
  619.5 41.2 %all-reduce.10 = (f32[2048]{0:T(1024)S(1)}, f32[2048]{0:T(1024)S(1)}, f32[2048]{0:T(1024)S(1)}) all-reduce(f32[2048]{0:T(1024)S(1)} %get-tuple-element.222, f32[2048]{0:T(1024)S(1)} %get-tuple-element.224, f32[2048]{0:T(1024)S(1)} %get-tuple-element.253), channel_id=4, replica_groups=mesh['fsdp'=8,'tp'=4] {'fsdp','tp'}, use_global_device_ids=true, to_apply=%region_12.13.clone | all-reduce | flops 6144 | bytes 49152
  661.9 51.6 %reduce-scatter.14.cloned.1.call-done = f32[3,256,512]{1,2,0:T(8,128)} async-done(((f32[3,2048,512]{1,2,0:T(8,128)}), f32[3,256,512]{1,2,0:T(8,128)}) %reduce-scatter.14.cloned.1.call-update) | async-done | bytes 1572880 | tf_op jit(solution)/shard_map/reduce_scatter | solution.py:273
  713.6 3.0 copy.78
  716.6 52.6 %reduce-scatter.16.cloned.1.call-done = f32[512,256]{1,0:T(8,128)} async-done(((f32[512,2048]{1,0:T(8,128)}), f32[512,256]{1,0:T(8,128)}) %reduce-scatter.16.cloned.1.call-update) | async-done | bytes 524304 | tf_op jit(solution)/shard_map/reduce_scatter | solution.py:275
  769.2 120.0 %reduce-scatter.18.cloned.1.call-done = f32[256,2048]{1,0:T(8,128)} async-done(((f32[2048,2048]{1,0:T(8,128)}), f32[256,2048]{1,0:T(8,128)}) %reduce-scatter.18.cloned.1.call-update) | async-done | bytes 2097168 | tf_op jit(solution)/shard_map/reduce_scatter | solution.py:276
  889.2 120.2 %reduce-scatter.20.cloned.1.call-done = f32[2048,256]{1,0:T(8,128)} async-done(((f32[2048,2048]{1,0:T(8,128)}), f32[2048,256]{1,0:T(8,128)}) %reduce-scatter.20.cloned.1.call-update) | async-done | bytes 2097168 | tf_op jit(solution)/shard_map/reduce_scatter | solution.py:278
  (166 shorter events, 31.5 us)
Async XLA Ops:
  7.2 56.0 %copy-start.21 = (s32[4096]{0:T(1024)S(1)}, s32[4096]{0:T(1024)}, u32[]{:S(2)}) copy-start(s32[4096]{0:T(1024)} %param.27) | copy-start | bytes 49156
  7.2 56.1 %copy-start.20 = (s32[4096]{0:T(1024)S(1)}, s32[4096]{0:T(1024)}, u32[]{:S(2)}) copy-start(s32[4096]{0:T(1024)} %param.29) | copy-start | bytes 49156
  7.2 56.3 %copy-start.29 = (s32[39,3]{0,1:T(4,128)S(1)}, s32[39,3]{0,1:T(4,128)}, u32[]{:S(2)}) copy-start(s32[39,3]{0,1:T(4,128)} %param.28) | copy-start | bytes 1408
  7.2 97.6 %all-gather.9.cloned.1.call-start = ((), (), s32[]{:S(2)}) async-start(), calls=%async_computation.7 | async-start | bytes 2621440 | tf_op jit(solution)/shard_map/all_gather | solution.py:136
  52.9 2.6 copy-start.16
  54.1 1.4 copy-start.22
  54.1 11.5 %copy-start.30 = (bf16[3,64]{1,0:T(4,128)(2,1)S(1)}, bf16[3,64]{1,0:T(4,128)(2,1)}, u32[]{:S(2)}) copy-start(bf16[3,64]{1,0:T(4,128)(2,1)} %param.19) | copy-start | bytes 1156
  54.1 21.8 %copy-start.34 = (bf16[256]{0:T(256)(128)(2,1)S(1)}, bf16[256]{0:T(256)(128)(2,1)}, u32[]{:S(2)}) copy-start(bf16[256]{0:T(256)(128)(2,1)} %param.23) | copy-start | bytes 1540
  55.5 8.2 copy-start.31
  55.5 0.5 copy-start.25
  58.3 94.3 %all-gather.11.cloned.1.call-start = ((), (), s32[]{:S(2)}) async-start(), calls=%async_computation.8 | async-start | bytes 7077888 | tf_op jit(solution)/shard_map/all_gather | solution.py:129
  60.7 139.5 %all-gather.19.cloned.1.call-start = ((), (), s32[]{:S(2)}) async-start(), calls=%async_computation.13 | async-start | bytes 2621440 | tf_op jit(solution)/shard_map/all_gather | solution.py:192
  61.4 167.5 %all-gather.13.cloned.1.call-start = ((), (), s32[]{:S(2)}) async-start(), calls=%async_computation.9 | async-start | bytes 2359296 | tf_op jit(solution)/shard_map/all_gather | solution.py:131
  62.0 337.9 %all-gather.15.cloned.1.call-start = ((), (), s32[]{:S(2)}) async-start(), calls=%async_computation.10 | async-start | bytes 9437184 | tf_op jit(solution)/shard_map/all_gather | solution.py:132
  62.6 357.7 %all-gather.17.cloned.1.call-start = ((), (), s32[]{:S(2)}) async-start(), calls=%async_computation.11 | async-start | bytes 9437184 | tf_op jit(solution)/shard_map/all_gather | solution.py:134
  63.1 446.8 %reduce-scatter.22.cloned.1.call-start = ((), (), s32[]{:S(2)}) async-start(), calls=%async_computation.19 | async-start | bytes 294912
  158.9 1.6 copy-start.4
  160.5 78.9 %copy-start.14 = (bf16[512,8,64]{0,2,1:T(8,128)(2,1)}, bf16[512,8,64]{0,2,1:T(8,128)(2,1)S(1)}, u32[]{:S(2)}) copy-start(bf16[512,8,64]{0,2,1:T(8,128)(2,1)S(1)} %maximum_convert_fusion) | copy-start | bytes 1572868
  160.6 78.8 %collective-permute-start.2 = (bf16[512,512]{0,1:T(8,128)(2,1)S(1)}, bf16[512,512]{0,1:T(8,128)(2,1)}, u32[]{:S(2)}, u32[]{:S(2)}) collective-permute-start(bf16[512,512]{0,1:T(8,128)(2,1)S(1)} %bitcast.97), channel_id=1, source_target_pairs={{0,8},{4,12},{8,16},{12,20},{16,24},{20,28},{1,9},{5,13},{9,17},{1... | collective-permute-start | bytes 1572872 | tf_op jit(solution)/shard_map/ppermute | solution.py:15
  164.7 74.7 %collective-permute-start.3 = (bf16[512,512]{0,1:T(8,128)(2,1)S(1)}, bf16[512,512]{0,1:T(8,128)(2,1)}, u32[]{:S(2)}, u32[]{:S(2)}) collective-permute-start(bf16[512,512]{0,1:T(8,128)(2,1)S(1)} %bitcast.98), channel_id=1, source_target_pairs={{0,4},{4,8},{8,12},{12,16},{16,20},{20,24},{24,28},{1,5},{5,9},{9,... | collective-permute-start | bytes 1572872 | tf_op jit(solution)/shard_map/ppermute | solution.py:15
  233.8 29.2 %collective-permute-start = (bf16[512,512]{0,1:T(8,128)(2,1)S(1)}, bf16[512,512]{0,1:T(8,128)(2,1)S(1)}, u32[]{:S(2)}, u32[]{:S(2)}) collective-permute-start(bf16[512,512]{0,1:T(8,128)(2,1)S(1)} %fusion.41), channel_id=1, source_target_pairs={{0,8},{4,12},{8,16},{12,20},{16,24},{20,28},{1,9},{5,13},{9,17},{1... | collective-permute-start | bytes 1572872 | tf_op jit(solution)/shard_map/ppermute | solution.py:15
  237.2 25.8 %collective-permute-start.1 = (bf16[512,512]{0,1:T(8,128)(2,1)S(1)}, bf16[512,512]{0,1:T(8,128)(2,1)S(1)}, u32[]{:S(2)}, u32[]{:S(2)}) collective-permute-start(bf16[512,512]{0,1:T(8,128)(2,1)S(1)} %fusion.41), channel_id=1, source_target_pairs={{0,4},{4,8},{8,12},{12,16},{16,20},{20,24},{24,28},{1,5},{5,9},{9,... | collective-permute-start | bytes 1572872 | tf_op jit(solution)/shard_map/ppermute | solution.py:15
  262.9 0.6 copy-start.18
  300.5 5.0 copy-start
  307.2 33.2 %collective-permute-start.4 = (f32[512,512]{0,1:T(8,128)}, f32[512,512]{0,1:T(8,128)}, u32[]{:S(2)}, u32[]{:S(2)}) collective-permute-start(f32[512,512]{0,1:T(8,128)} %bitcast.23), channel_id=1, source_target_pairs={{4,0},{8,4},{12,8},{16,12},{20,16},{24,20},{28,24},{5,1},{9,5},{13... | collective-permute-start | bytes 3145736 | tf_op jit(solution)/shard_map/ppermute | solution.py:15
  308.5 54.5 %collective-permute-start.5 = (f32[512,512]{0,1:T(8,128)}, f32[512,512]{0,1:T(8,128)}, u32[]{:S(2)}, u32[]{:S(2)}) collective-permute-start(f32[512,512]{0,1:T(8,128)} %bitcast.24), channel_id=1, source_target_pairs={{8,0},{12,4},{16,8},{20,12},{24,16},{28,20},{9,1},{13,5},{17,9},{2... | collective-permute-start | bytes 3145736 | tf_op jit(solution)/shard_map/ppermute | solution.py:15
  324.9 49.4 %collective-permute-start.6 = (f32[512,512]{1,0:T(8,128)}, f32[512,512]{1,0:T(8,128)}, u32[]{:S(2)}, u32[]{:S(2)}) collective-permute-start(f32[512,512]{1,0:T(8,128)} %copy.71), channel_id=1, source_target_pairs={{4,0},{8,4},{12,8},{16,12},{20,16},{24,20},{28,24},{5,1},{9,5},{13... | collective-permute-start | bytes 3145736 | tf_op jit(solution)/shard_map/ppermute | solution.py:15
  327.5 58.6 %collective-permute-start.7 = (f32[512,512]{1,0:T(8,128)}, f32[512,512]{1,0:T(8,128)}, u32[]{:S(2)}, u32[]{:S(2)}) collective-permute-start(f32[512,512]{1,0:T(8,128)} %copy.73), channel_id=1, source_target_pairs={{8,0},{12,4},{16,8},{20,12},{24,16},{28,20},{9,1},{13,5},{17,9},{2... | collective-permute-start | bytes 3145736 | tf_op jit(solution)/shard_map/ppermute | solution.py:15
  337.7 1.1 copy-start.2
  340.4 25.6 %copy-start.3 = (f32[512,8,64]{0,2,1:T(8,128)S(1)}, f32[512,8,64]{0,2,1:T(8,128)}, u32[]{:S(2)}) copy-start(f32[512,8,64]{0,2,1:T(8,128)} %copy-done.2) | copy-start | bytes 3145732
  340.4 27.2 %copy-start.15 = (bf16[512,8,32]{0,2,1:T(8,128)(2,1)S(1)}, bf16[512,8,32]{0,2,1:T(8,128)(2,1)}, u32[]{:S(2)}) copy-start(bf16[512,8,32]{0,2,1:T(8,128)(2,1)} %slice.201) | copy-start | bytes 786436
  387.9 0.8 copy-start.5
  391.0 29.2 %copy-start.24 = (f32[8,1,256]{2,1,0:T(1,128)S(1)}, f32[8,1,256]{2,1,0:T(1,128)}, u32[]{:S(2)}) copy-start(f32[8,1,256]{2,1,0:T(1,128)} %convert_element_type.155) | copy-start | bytes 24580
  391.0 145.7 %reduce-scatter.12.cloned.1.call-start = ((), (), s32[]{:S(2)}) async-start(), calls=%async_computation.14 | async-start | bytes 5242880 | tf_op jit(solution)/shard_map/reduce_scatter | solution.py:268
  420.2 12.3 %copy-start.33 = (bf16[2048,2048]{1,0:T(8,128)(2,1)S(1)}, bf16[2048,2048]{1,0:T(8,128)(2,1)}, u32[]{:S(2)}) copy-start(bf16[2048,2048]{1,0:T(8,128)(2,1)} %all-gather.15.cloned.1.call-done) | copy-start | bytes 25165828
  432.5 4.8 copy-start.37
  432.5 4.8 copy-start.6
  432.5 4.8 copy-start.7
  432.5 4.8 copy-start.9
  445.2 0.7 copy-start.19
  445.3 171.0 %reduce-scatter.10.cloned.1.call-start = ((), (), s32[]{:S(2)}) async-start(), calls=%async_computation.12 | async-start | bytes 5242880 | tf_op jit(solution)/shard_map/reduce_scatter | solution.py:189
  446.0 11.6 %copy-start.38 = (f32[512,2048]{1,0:T(8,128)S(1)}, f32[512,2048]{1,0:T(8,128)}, u32[]{:S(2)}) copy-start(f32[512,2048]{1,0:T(8,128)} %fusion.61) | copy-start | bytes 12582916
  457.6 8.1 copy-start.13
  469.1 1.0 copy-start.8
  469.1 1.2 copy-start.10
  469.1 244.5 %reduce-scatter.14.cloned.1.call-start = ((), (), s32[]{:S(2)}) async-start(), calls=%async_computation.15 | async-start | bytes 14155776 | tf_op jit(solution)/shard_map/reduce_scatter | solution.py:273
  478.3 1.6 copy-start.11
  478.3 290.9 %reduce-scatter.16.cloned.1.call-start = ((), (), s32[]{:S(2)}) async-start(), calls=%async_computation.16 | async-start | bytes 4718592 | tf_op jit(solution)/shard_map/reduce_scatter | solution.py:275
  483.2 406.1 %reduce-scatter.18.cloned.1.call-start = ((), (), s32[]{:S(2)}) async-start(), calls=%async_computation.17 | async-start | bytes 18874368 | tf_op jit(solution)/shard_map/reduce_scatter | solution.py:276
  496.1 513.3 %reduce-scatter.20.cloned.1.call-start = ((), (), s32[]{:S(2)}) async-start(), calls=%async_computation.18 | async-start | bytes 18874368 | tf_op jit(solution)/shard_map/reduce_scatter | solution.py:278
  508.0 0.7 copy-start.35
  508.0 1.9 copy-start.27
  508.0 1.9 copy-start.28
  508.0 28.7 %copy-start.1 = (bf16[128,2048]{1,0:T(8,128)(2,1)S(1)}, bf16[128,2048]{1,0:T(8,128)(2,1)}, u32[]{:S(2)}) copy-start(bf16[128,2048]{1,0:T(8,128)(2,1)} %param.15) | copy-start | bytes 1572868
  508.0 28.7 %copy-start.17 = (f32[2048]{0:T(1024)S(1)}, f32[2048]{0:T(1024)}, u32[]{:S(2)}) copy-start(f32[2048]{0:T(1024)} %copy-done.16) | copy-start | bytes 24580
  508.0 28.7 %copy-start.23 = (f32[128]{0:T(128)S(1)}, f32[128]{0:T(128)}, u32[]{:S(2)}) copy-start(f32[128]{0:T(128)} %copy-done.22) | copy-start | bytes 1540
  508.0 30.2 %copy-start.32 = (f32[128]{0:T(128)S(1)}, f32[128]{0:T(128)}, u32[]{:S(2)}) copy-start(f32[128]{0:T(128)} %copy-done.31) | copy-start | bytes 1540
  508.0 30.2 %copy-start.26 = (f32[128]{0:T(128)S(1)}, f32[128]{0:T(128)}, u32[]{:S(2)}) copy-start(f32[128]{0:T(128)} %copy-done.25) | copy-start | bytes 1540
  508.1 108.2 %copy-start.12 = (bf16[128,2048]{1,0:T(8,128)(2,1)S(1)}, bf16[128,2048]{1,0:T(8,128)(2,1)}, u32[]{:S(2)}) copy-start(bf16[128,2048]{1,0:T(8,128)(2,1)} %param.26) | copy-start | bytes 1572868
  660.7 349.2 %copy-start.36 = (f32[64]{0:T(128)}, f32[64]{0:T(128)S(1)}, u32[]{:S(2)}) copy-start(f32[64]{0:T(128)S(1)} %dynamic-slice.2) | copy-start | bytes 772
Sparse Core Ops, SparseCore 0:
  58.4 46.3 all-gather.8
  107.2 45.3 all-gather.10
  154.2 45.9 all-gather.18
  201.9 26.8 all-gather.12
  230.6 64.4 all-gather.14
  296.8 123.3 all-gather.16
  423.8 33.6 reduce-scatter.21
  459.9 76.7 reduce-scatter.11
  539.0 77.2 reduce-scatter.9
  620.0 93.4 reduce-scatter.13
  717.9 51.3 reduce-scatter.15
  773.2 115.9 reduce-scatter.17
  893.4 115.9 reduce-scatter.19
where the time goes:
time: 1020 us
  waiting for transfers between devices  607 us (60%)
  matrix products  158 us (15%)
  blocking collectives  116 us (11%)
  other arithmetic  54 us (5%)
  local copies, waits for them, and re-layouts  40 us (4%)
  starting transfers between devices  27.1 us (3%)
  between operations  15.8 us (2%)
    reduce_scatter x1, waiting for transfers between devices, body(): lax.psum_scatter(outer_grad, 'fsdp', scatter_dimension=1, tiled=True)  120 us
    reduce_scatter x1, waiting for transfers between devices, body(): lax.psum_scatter(inner_grad, 'fsdp', scatter_dimension=0, tiled=True)  120 us
    unnamed x3, blocking collectives  97.5 us
    reduce_scatter x1, waiting for transfers between devices, body(): lax.psum_scatter(partial_rows, 'tp', scatter_dimension=0, tiled=True)  76.3 us
    reduce_scatter x1, waiting for transfers between devices, body(): lax.psum_scatter(dense_grad, 'fsdp', scatter_dimension=1, tiled=True)  52.6 us
    reduce_scatter x1, waiting for transfers between devices, body(): lax.psum_scatter(qkv_weight_part, 'fsdp', scatter_dimension=1, tiled=True)  51.6 us
    all_gather x1, waiting for transfers between devices, forward_pieces(): lax.all_gather(qkv_weight, 'fsdp', axis=1, tiled=True)  47.9 us
    ppermute x8, waiting for transfers between devices, passed_along(): lax.ppermute(value, axis, [(source, source + steps) for source in range(i...  34.4 us
  transfers between devices with their start and end apart: 21, of which 13 were waited for; matrix products, arithmetic and copies ran while one was open for 23% of the time, Pallas kernels for 0%

commit v1 on v0

--- a/solution.py
+++ b/solution.py
@@ -189,7 +189,13 @@
     summed_rows = lax.psum_scatter(partial_rows, "tp", scatter_dimension=0, tiled=True)
     output = (inputs_f + summed_rows + bias_sum).astype(bf16)
     out_bias_grad = jnp.sum(cotangent.astype(f32), axis=0)
-    grad_rows = lax.all_gather(cotangent, "tp", axis=0, tiled=True)
+    count_2 = lax.axis_size("tp")
+    held, blocks = (cotangent, [cotangent])
+    for _ in range(count_2 - 1):
+        held = lax.ppermute(held, "tp", [(i, (i + 1) % count_2) for i in range(count_2)])
+        blocks.insert(0, held)
+    line = jnp.concatenate(blocks, axis=0)
+    grad_rows = jnp.roll(line, (lax.axis_index("tp") + 1) * cotangent.shape[0], axis=0)
     gathered, normed, queries, keys_win, values_win, attended, log_sums, pre_act, activated = (
         forward_pieces()
     )

time: 1020 us -> 1000 us (0.980)
  waiting for transfers between devices: 607 us -> 563 us
  starting transfers between devices: 27.1 us -> 41 us
    ppermute x0 -> x3, waiting for transfers between devices: none -> 34.3 us  [body(): lax.ppermute(held, 'tp', [(i, (i + 1) % count_2) for i in range(count_2)])]
    all_gather x1 -> x0, waiting for transfers between devices: 32.8 us -> none  [body(): grad_rows = lax.all_gather(cotangent, 'tp', axis=0, tiled=True)]
    all_gather x1, waiting for transfers between devices: 19.4 us -> 0.01 us  [forward_pieces(): normed = lax.all_gather(normed_local, 'tp', axis=0, tiled=True)]
    all_gather x1, waiting for transfers between devices: 47.9 us -> 30.4 us  [forward_pieces(): lax.all_gather(qkv_weight, 'fsdp', axis=1, tiled=True)]
    ppermute x0 -> x3, starting transfers between devices: none -> 15.1 us  [body(): lax.ppermute(held, 'tp', [(i, (i + 1) % count_2) for i in range(count_2)])]
    all_gather x1, waiting for transfers between devices: 9.85 us -> 20.7 us  [forward_pieces(): lax.all_gather(outer_weight, 'fsdp', axis=1, tiled=True)]
    unnamed x97 -> x106, local copies, waits for them, and re-layouts: 23.9 us -> 29.1 us
  transfers between devices with their start and end apart: 21 -> 23, of which waited for: 13 -> 14; matrix products, arithmetic and copies ran while one was open for 23% -> 24% of each run, Pallas kernels for 0% -> 0%
where the time goes in v1:
time: 1000 us; the launch traced here: 995 us
  waiting for transfers between devices  563 us (56%)
  matrix products  159 us (16%)
  blocking collectives  116 us (12%)
  other arithmetic  54.1 us (5%)
  local copies, waits for them, and re-layouts  46 us (5%)
  starting transfers between devices  41 us (4%)
  between operations  16.1 us (2%)
    reduce_scatter x1, waiting for transfers between devices, body(): lax.psum_scatter(outer_grad, 'fsdp', scatter_dimension=1, tiled=True)  120 us
    reduce_scatter x1, waiting for transfers between devices, body(): lax.psum_scatter(inner_grad, 'fsdp', scatter_dimension=0, tiled=True)  120 us
    unnamed x3, blocking collectives  97.5 us
    reduce_scatter x1, waiting for transfers between devices, body(): lax.psum_scatter(partial_rows, 'tp', scatter_dimension=0, tiled=True)  76.2 us
    reduce_scatter x1, waiting for transfers between devices, body(): lax.psum_scatter(dense_grad, 'fsdp', scatter_dimension=1, tiled=True)  52.5 us
    reduce_scatter x1, waiting for transfers between devices, body(): lax.psum_scatter(qkv_weight_part, 'fsdp', scatter_dimension=1, tiled=True)  51.8 us
    ppermute x3, waiting for transfers between devices, body(): lax.ppermute(held, 'tp', [(i, (i + 1) % count_2) for i in range(count_2)])  34.3 us
    all_gather x1, waiting for transfers between devices, forward_pieces(): lax.all_gather(qkv_weight, 'fsdp', axis=1, tiled=True)  30.4 us
  transfers between devices with their start and end apart: 23, of which 14 were waited for; matrix products, arithmetic and copies ran while one was open for 24% of the time, Pallas kernels for 0%

profile of v1, /device:TPU:0, one launch (start us, length us, event | category | flops | bytes accessed | tf_op | source)
XLA Modules:
  0.0 994.8 jit_solution(17308605548834277114)
XLA Ops:
  10.8 42.2 %all-reduce.11 = (bf16[2048]{0:T(1024)(128)(2,1)S(1)}, bf16[2048]{0:T(1024)(128)(2,1)S(1)}, bf16[2048]{0:T(1024)(128)(2,1)}, bf16[2048]{0:T(1024)(128)(2,1)}) all-reduce(bf16[2048]{0:T(1024)(128)(2,1)S(1)} %dynamic-update-slice.1, bf16[2048]{0:T(1024)(128)(2,1)S(1)} %dynamic-update-slice, ...), channel_id=1, replica_groups=mesh['fsdp'=8,'tp'=4] {'fsdp','tp'}, use_global_device_ids=true, to_apply=%add.3 | all-reduce | flops 8192 | bytes 32768
  55.6 2.2 fusion.44
  57.9 2.3 copy.69
  61.6 1.6 collective-permute-start.4
  63.6 10.2 %all-gather = bf16[8,64,3]{1,2,0:T(4,128)(2,1)S(1)} all-gather(bf16[1,64,3]{1,2,0:T(4,128)(2,1)S(1)} %bitcast.106), channel_id=1, replica_groups=mesh['fsdp'=8,'tp'=4] {'fsdp'}, dimensions={0}, use_global_device_ids=true | all-gather | bytes 3456 | tf_op jit(solution)/shard_map/all_gather | solution.py:130
  73.9 7.9 all-gather.1
  82.6 1.9 collective-permute-done.4
  84.5 7.1 collective-permute-start.5
  91.6 1.8 convert_reduce_fusion.2
  93.5 20.9 %collective-permute-done.5 = bf16[128,2048]{1,0:T(8,128)(2,1)S(1)} collective-permute-done((bf16[128,2048]{1,0:T(8,128)(2,1)S(1)}, bf16[128,2048]{1,0:T(8,128)(2,1)S(1)}, u32[]{:S(2)}, u32[]{:S(2)}) %collective-permute-start.5) | collective-permute-done | bytes 524320 | tf_op jit(solution)/shard_map/ppermute | solution.py:195
  114.4 6.5 collective-permute-start.6
  121.8 11.4 %collective-permute-done.6 = bf16[128,2048]{1,0:T(8,128)(2,1)S(1)} collective-permute-done((bf16[128,2048]{1,0:T(8,128)(2,1)S(1)}, bf16[128,2048]{1,0:T(8,128)(2,1)S(1)}, u32[]{:S(2)}, u32[]{:S(2)}) %collective-permute-start.6) | collective-permute-done | bytes 524320 | tf_op jit(solution)/shard_map/ppermute | solution.py:195
  140.0 30.4 %all-gather.10.cloned.1.call-done = bf16[3,2048,512]{1,2,0:T(8,128)(2,1)} async-done(((bf16[3,256,512]{1,2,0:T(8,128)(2,1)}), bf16[3,2048,512]{1,2,0:T(8,128)(2,1)}) %all-gather.10.cloned.1.call-update) | async-done | bytes 6291472 | tf_op jit(solution)/shard_map/all_gather | solution.py:129
  170.5 6.2 add_bitcast_fusion
  178.4 4.2 collective-permute-start.2
  182.5 2.7 collective-permute-start.3
  185.2 20.9 %all-gather.12.cloned.1.call-done = bf16[512,2048]{1,0:T(8,128)(2,1)} async-done(((bf16[512,256]{1,0:T(8,128)(2,1)}), bf16[512,2048]{1,0:T(8,128)(2,1)}) %all-gather.12.cloned.1.call-update) | async-done | bytes 2097168 | tf_op jit(solution)/shard_map/all_gather | solution.py:131
  206.2 3.5 fusion.37
  211.1 2.3 collective-permute-start
  213.4 2.2 collective-permute-start.1
  215.6 12.0 %select_reduce_fusion = (f32[8,512]{1,0:T(8,128)S(1)}, f32[8,512,1536]{2,1,0:T(8,128)}) fusion(pred[512,1536]{1,0:T(8,128)(4,1)S(1)} %get-tuple-element.234, bf16[512,8,64]{0,2,1:T(8,128)(2,1)S(1)} %maximum_convert_fusion, bf16[512,8,64]{0,2,1:T(8,128)(2,1)} %bitcast.14, bf16[512,8,64]{0,2,1:T(8,128)(2,1)} %bitcast.13, bf16[512,8,32]{0,2,1:T(8,128)(2,1)S(1)} %slice.202, ...), kind=kOutput, calls=%fused_computation.5 | convolution fusion | flops 830468096 | bytes 28065792 | tf_op jit(solution)/shard_map/while/body/eval_jaxpr/qhe,khe->hqk/dot_general | solution.py:157
  227.5 11.6 %fusion = f32[8,512]{1,0:T(8,128)S(1)} fusion(f32[8,512,1536]{2,1,0:T(8,128)} %get-tuple-element.266, f32[8,512]{1,0:T(8,128)S(1)} %get-tuple-element.265, pred[512,1536]{1,0:T(8,128)(4,1)S(1)} %get-tuple-element.234), kind=kLoop, calls=%fused_computation.6 | loop fusion | flops 25161728 | bytes 25985024 | tf_op jit(solution)/shard_map/while/body/eval_jaxpr/reduce_sum | solution.py:162
  239.7 19.6 %multiply_reduce_fusion = (f32[8,512]{1,0:T(8,128)S(1)}, f32[8,512,1536]{2,1,0:T(8,128)}) fusion(f32[8,512,1536]{2,1,0:T(8,128)} %get-tuple-element.266, f32[8,512]{1,0:T(8,128)S(1)} %log_add_fusion, pred[512,1536]{1,0:T(8,128)(4,1)S(1)} %get-tuple-element.234, bf16[512,8,64]{0,2,1:T(8,128)(2,1)S(1)} %bitcast.96, bf16[1536,8,64]{0,2,1:T(8,128)(2,1)S(1)} %bitcast.78), kind=kOutput, calls=%fused_computation.1 | convolution fusion | flops 836759552 | bytes 53248000 | tf_op jit(solution)/shard_map/while/body/eval_jaxpr/qhe,khe->hqk/dot_general | solution.py:228
  259.3 17.5 %multiply_convert_fusion = bf16[8,512,1536]{2,1,0:T(8,128)(2,1)S(1)} fusion(f32[8,512,1536]{2,1,0:T(8,128)} %get-tuple-element.268, f32[8,512,1536]{2,1,0:T(8,128)} %get-tuple-element.266, f32[8,512]{1,0:T(8,128)S(1)} %get-tuple-element.267, f32[8,512]{1,0:T(8,128)S(1)} %log_add_fusion, pred[512,1536]{1,0:T(8,128)(4,1)S(1)} %get-tuple-element.234), kind=kLoop, calls=%fused_computation | loop fusion | flops 37748736 | bytes 63733760 | tf_op jit(solution)/shard_map/while/body/eval_jaxpr/convert_element_type | solution.py:230
  276.8 2.3 fusion.13
  279.1 2.3 copy-done
  281.4 1.7 fusion.72
  285.7 10.9 %fusion.14 = f32[1536,8,64]{0,2,1:T(8,128)S(1)} fusion(bf16[512,8,64]{0,2,1:T(8,128)(2,1)S(1)} %bitcast.97, f32[8,512,1536]{2,1,0:T(8,128)} %get-tuple-element.266, f32[8,512]{1,0:T(8,128)S(1)} %log_add_fusion, pred[512,1536]{1,0:T(8,128)(4,1)S(1)} %get-tuple-element.234), kind=kOutput, calls=%fused_computation.26 | convolution fusion | flops 830472192 | bytes 29638656 | tf_op jit(solution)/shard_map/while/body/eval_jaxpr/hqk,qhe->khe/dot_general | solution.py:238
  296.6 1.6 fusion.73
  298.3 2.5 copy.73
  304.7 9.0 fusion.26
  314.7 1.6 copy.72
  316.3 24.3 %collective-permute-done.8 = f32[512,512]{0,1:T(8,128)} collective-permute-done((f32[512,512]{0,1:T(8,128)}, f32[512,512]{0,1:T(8,128)}, u32[]{:S(2)}, u32[]{:S(2)}) %collective-permute-start.8) | collective-permute-done | bytes 1048608 | tf_op jit(solution)/shard_map/ppermute | solution.py:15
  340.6 2.2 fusion.51
  343.6 1.6 subtract_convert_fusion.1
  346.0 2.0 copy.74
  348.1 1.8 pad_maximum_fusion.7
  349.9 2.0 copy.75
  352.6 1.8 fusion.53
  357.5 8.8 reduce-scatter.12.cloned.1.call-start
  366.4 10.9 %fusion.76 = f32[512,2048]{1,0:T(8,128)} fusion(bf16[512,2048]{1,0:T(8,128)(2,1)} %all-gather.8.cloned.1.call-done, bf16[2048,2048]{1,0:T(8,128)(2,1)} %all-gather.14.cloned.1.call-done), kind=kOutput, calls=%fused_computation.142 | convolution fusion | flops 4294967296 | bytes 14680064 | tf_op jit(solution)/shard_map/dot_general | solution.py:169
  377.3 20.7 %all-gather.16.cloned.1.call-done = bf16[2048,2048]{1,0:T(8,128)(2,1)} async-done(((bf16[2048,256]{1,0:T(8,128)(2,1)}), bf16[2048,2048]{1,0:T(8,128)(2,1)}) %all-gather.16.cloned.1.call-update) | async-done | bytes 8388624 | tf_op jit(solution)/shard_map/all_gather | solution.py:134
  398.0 12.2 %convert_reduce_fusion = (f32[2048]{0:T(1024)S(1)}, bf16[512,2048]{1,0:T(8,128)(2,1)S(1)}) fusion(f32[512,2048]{1,0:T(8,128)} %fusion.76, f32[2048]{0:T(1024)S(1)} %bitcast.102, bf16[2048,2048]{1,0:T(8,128)(2,1)} %all-gather.16.cloned.1.call-done, bf16[1024,2048]{1,0:T(8,128)(2,1)} %constant_dynamic-update-slice_fusion, s32[]{:T(128)S(6)} %select_n.36), kind=kOutput, calls=%fused_computation.22 | convolution fusion | flops 4319082496 | bytes 16793604 | tf_op jit(solution)/shard_map/td,fd->tf/dot_general | solution.py:207
  410.3 4.8 fusion.77
  415.1 7.9 bitcast_add_fusion
  423.7 11.6 %fusion.40 = bf16[8,64,512]{2,1,0:T(8,128)(2,1)S(1)} fusion(bf16[1536,8,64]{0,2,1:T(8,128)(2,1)S(1)} %bitcast.79, f32[8,512,1536]{2,1,0:T(8,128)} %get-tuple-element.266, f32[8,512]{1,0:T(8,128)S(1)} %copy-done.19, f32[8,512]{1,0:T(8,128)S(1)} %get-tuple-element.265, pred[512,1536]{1,0:T(8,128)(4,1)S(1)} %get-tuple-element.234), kind=kOutput, calls=%fused_computation.59 | convolution fusion | flops 837025792 | bytes 28082176 | tf_op jit(solution)/shard_map/while/body/eval_jaxpr/hqk,khe->qhe/dot_general | solution.py:164
  435.3 8.1 fusion.70
  443.4 3.4 convolution_add_fusion
  448.0 7.9 convolution_bitcast_fusion
  456.0 4.9 fusion.29
  461.2 14.0 %fusion.27 = f32[2048,2048]{1,0:T(8,128)} fusion(bf16[1024,2048]{1,0:T(8,128)(2,1)} %constant_dynamic-update-slice_fusion, s32[]{:T(128)S(6)} %select_n.36, f32[512,2048]{1,0:T(8,128)} %fusion.76, f32[2048]{0:T(1024)S(1)} %bitcast.104), kind=kOutput, calls=%fused_computation.48 | convolution fusion | flops 4305453056 | bytes 23076868 | tf_op jit(solution)/shard_map/tf,td->fd/dot_general | solution.py:206
  476.8 9.8 fusion.78
  489.9 14.1 %all-reduce.9 = f32[2048]{0:T(1024)S(1)} all-reduce(f32[2048]{0:T(1024)S(1)} %get-tuple-element.269), channel_id=11, replica_groups=mesh['fsdp'=8,'tp'=4] {'fsdp'}, use_global_device_ids=true, to_apply=%region_23.24.clone | all-reduce | flops 2048 | bytes 16384
  504.6 9.6 reduce-scatter.12.cloned.1.call-done
  514.3 1.6 fusion.71
  515.9 1.7 fusion.45
  517.6 76.2 %reduce-scatter.10.cloned.1.call-done = f32[128,2048]{1,0:T(8,128)} async-done(((f32[512,2048]{1,0:T(8,128)}), f32[128,2048]{1,0:T(8,128)}) %reduce-scatter.10.cloned.1.call-update) | async-done | bytes 1048592 | tf_op jit(solution)/shard_map/reduce_scatter | solution.py:189
  593.9 3.2 convert_reduce_fusion.4
  597.0 41.2 %all-reduce.10 = (f32[2048]{0:T(1024)S(1)}, f32[2048]{0:T(1024)S(1)}, f32[2048]{0:T(1024)S(1)}) all-reduce(f32[2048]{0:T(1024)S(1)} %get-tuple-element.222, f32[2048]{0:T(1024)S(1)} %get-tuple-element.224, f32[2048]{0:T(1024)S(1)} %get-tuple-element.251), channel_id=4, replica_groups=mesh['fsdp'=8,'tp'=4] {'fsdp','tp'}, use_global_device_ids=true, to_apply=%region_12.13.clone | all-reduce | flops 6144 | bytes 49152
  639.5 51.8 %reduce-scatter.14.cloned.1.call-done = f32[3,256,512]{1,2,0:T(8,128)} async-done(((f32[3,2048,512]{1,2,0:T(8,128)}), f32[3,256,512]{1,2,0:T(8,128)}) %reduce-scatter.14.cloned.1.call-update) | async-done | bytes 1572880 | tf_op jit(solution)/shard_map/reduce_scatter | solution.py:279
  691.3 3.0 copy.78
  694.4 52.5 %reduce-scatter.16.cloned.1.call-done = f32[512,256]{1,0:T(8,128)} async-done(((f32[512,2048]{1,0:T(8,128)}), f32[512,256]{1,0:T(8,128)}) %reduce-scatter.16.cloned.1.call-update) | async-done | bytes 524304 | tf_op jit(solution)/shard_map/reduce_scatter | solution.py:281
  746.8 120.2 %reduce-scatter.20.cloned.1.call-done = f32[2048,256]{1,0:T(8,128)} async-done(((f32[2048,2048]{1,0:T(8,128)}), f32[2048,256]{1,0:T(8,128)}) %reduce-scatter.20.cloned.1.call-update) | async-done | bytes 2097168 | tf_op jit(solution)/shard_map/reduce_scatter | solution.py:284
  867.0 120.0 %reduce-scatter.18.cloned.1.call-done = f32[256,2048]{1,0:T(8,128)} async-done(((f32[2048,2048]{1,0:T(8,128)}), f32[256,2048]{1,0:T(8,128)}) %reduce-scatter.18.cloned.1.call-update) | async-done | bytes 2097168 | tf_op jit(solution)/shard_map/reduce_scatter | solution.py:282
  (179 shorter events, 41.8 us)
Async XLA Ops:
  7.2 54.4 %copy-start.2 = (bf16[128,2048]{1,0:T(8,128)(2,1)S(1)}, bf16[128,2048]{1,0:T(8,128)(2,1)}, u32[]{:S(2)}) copy-start(bf16[128,2048]{1,0:T(8,128)(2,1)} %param.26) | copy-start | bytes 1572868
  7.2 56.1 %copy-start.21 = (s32[4096]{0:T(1024)S(1)}, s32[4096]{0:T(1024)}, u32[]{:S(2)}) copy-start(s32[4096]{0:T(1024)} %param.27) | copy-start | bytes 49156
  7.2 56.2 %copy-start.20 = (s32[4096]{0:T(1024)S(1)}, s32[4096]{0:T(1024)}, u32[]{:S(2)}) copy-start(s32[4096]{0:T(1024)} %param.29) | copy-start | bytes 49156
  7.2 56.4 %copy-start.30 = (bf16[3,64]{1,0:T(4,128)(2,1)S(1)}, bf16[3,64]{1,0:T(4,128)(2,1)}, u32[]{:S(2)}) copy-start(bf16[3,64]{1,0:T(4,128)(2,1)} %param.19) | copy-start | bytes 1156
  7.2 66.7 %copy-start.35 = (bf16[256]{0:T(256)(128)(2,1)S(1)}, bf16[256]{0:T(256)(128)(2,1)}, u32[]{:S(2)}) copy-start(bf16[256]{0:T(256)(128)(2,1)} %param.23) | copy-start | bytes 1540
  7.2 75.2 %copy-start.29 = (s32[39,3]{0,1:T(4,128)S(1)}, s32[39,3]{0,1:T(4,128)}, u32[]{:S(2)}) copy-start(s32[39,3]{0,1:T(4,128)} %param.28) | copy-start | bytes 1408
  7.2 132.8 %all-gather.8.cloned.1.call-start = ((), (), s32[]{:S(2)}) async-start(), calls=%async_computation.7 | async-start | bytes 2621440 | tf_op jit(solution)/shard_map/all_gather | solution.py:136
  53.0 2.6 copy-start.16
  54.2 37.4 %copy-start.22 = (f32[128]{0:T(128)}, f32[128]{0:T(128)S(1)}, u32[]{:S(2)}) copy-start(f32[128]{0:T(128)S(1)} %broadcast_multiply_fusion.1) | copy-start | bytes 1540
  55.6 18.3 %copy-start.31 = (f32[128]{0:T(128)}, f32[128]{0:T(128)S(1)}, u32[]{:S(2)}) copy-start(f32[128]{0:T(128)S(1)} %fusion.47) | copy-start | bytes 1540
  55.6 7.7 copy-start.25
  57.9 112.6 %all-gather.10.cloned.1.call-start = ((), (), s32[]{:S(2)}) async-start(), calls=%async_computation.8 | async-start | bytes 7077888 | tf_op jit(solution)/shard_map/all_gather | solution.py:129
  60.2 145.9 %all-gather.12.cloned.1.call-start = ((), (), s32[]{:S(2)}) async-start(), calls=%async_computation.9 | async-start | bytes 2359296 | tf_op jit(solution)/shard_map/all_gather | solution.py:131
  61.0 305.4 %all-gather.14.cloned.1.call-start = ((), (), s32[]{:S(2)}) async-start(), calls=%async_computation.10 | async-start | bytes 9437184 | tf_op jit(solution)/shard_map/all_gather | solution.py:132
  61.5 336.4 %all-gather.16.cloned.1.call-start = ((), (), s32[]{:S(2)}) async-start(), calls=%async_computation.11 | async-start | bytes 9437184 | tf_op jit(solution)/shard_map/all_gather | solution.py:134
  61.6 22.9 %collective-permute-start.4 = (bf16[128,2048]{1,0:T(8,128)(2,1)S(1)}, bf16[128,2048]{1,0:T(8,128)(2,1)S(1)}, u32[]{:S(2)}, u32[]{:S(2)}) collective-permute-start(bf16[128,2048]{1,0:T(8,128)(2,1)S(1)} %copy-done.2), channel_id=1, source_target_pairs={{0,1},{1,2},{2,3},{3,0},{4,5},{5,6},{6,7},{7,4},{8,9},{9,10},{10,1... | collective-permute-start | bytes 1572872 | tf_op jit(solution)/shard_map/ppermute | solution.py:195
  63.2 425.3 %reduce-scatter.22.cloned.1.call-start = ((), (), s32[]{:S(2)}) async-start(), calls=%async_computation.18 | async-start | bytes 294912
  84.5 29.9 %collective-permute-start.5 = (bf16[128,2048]{1,0:T(8,128)(2,1)S(1)}, bf16[128,2048]{1,0:T(8,128)(2,1)S(1)}, u32[]{:S(2)}, u32[]{:S(2)}) collective-permute-start(bf16[128,2048]{1,0:T(8,128)(2,1)S(1)} %collective-permute-done.4), channel_id=1, source_target_pairs={{0,1},{1,2},{2,3},{3,0},{4,5},{5,6},{6,7},{7,4},{8,9},{9,10},{10,1... | collective-permute-start | bytes 1572872 | tf_op jit(solution)/shard_map/ppermute | solution.py:195
  114.4 18.8 %collective-permute-start.6 = (bf16[128,2048]{1,0:T(8,128)(2,1)S(1)}, bf16[128,2048]{1,0:T(8,128)(2,1)S(1)}, u32[]{:S(2)}, u32[]{:S(2)}) collective-permute-start(bf16[128,2048]{1,0:T(8,128)(2,1)S(1)} %collective-permute-done.5), channel_id=1, source_target_pairs={{0,1},{1,2},{2,3},{3,0},{4,5},{5,6},{6,7},{7,4},{8,9},{9,10},{10,1... | collective-permute-start | bytes 1572872 | tf_op jit(solution)/shard_map/ppermute | solution.py:195
  176.7 1.6 copy-start.6
  178.4 37.2 %copy-start.14 = (bf16[512,8,64]{0,2,1:T(8,128)(2,1)}, bf16[512,8,64]{0,2,1:T(8,128)(2,1)S(1)}, u32[]{:S(2)}) copy-start(bf16[512,8,64]{0,2,1:T(8,128)(2,1)S(1)} %maximum_convert_fusion) | copy-start | bytes 1572868
  178.4 37.1 %collective-permute-start.2 = (bf16[512,512]{0,1:T(8,128)(2,1)S(1)}, bf16[512,512]{0,1:T(8,128)(2,1)}, u32[]{:S(2)}, u32[]{:S(2)}) collective-permute-start(bf16[512,512]{0,1:T(8,128)(2,1)S(1)} %bitcast.93), channel_id=1, source_target_pairs={{0,8},{4,12},{8,16},{12,20},{16,24},{20,28},{1,9},{5,13},{9,17},{1... | collective-permute-start | bytes 1572872 | tf_op jit(solution)/shard_map/ppermute | solution.py:15
  182.5 33.0 %collective-permute-start.3 = (bf16[512,512]{0,1:T(8,128)(2,1)S(1)}, bf16[512,512]{0,1:T(8,128)(2,1)}, u32[]{:S(2)}, u32[]{:S(2)}) collective-permute-start(bf16[512,512]{0,1:T(8,128)(2,1)S(1)} %bitcast.94), channel_id=1, source_target_pairs={{0,4},{4,8},{8,12},{12,16},{16,20},{20,24},{24,28},{1,5},{5,9},{9,... | collective-permute-start | bytes 1572872 | tf_op jit(solution)/shard_map/ppermute | solution.py:15
  211.1 28.1 %collective-permute-start = (bf16[512,512]{0,1:T(8,128)(2,1)S(1)}, bf16[512,512]{0,1:T(8,128)(2,1)S(1)}, u32[]{:S(2)}, u32[]{:S(2)}) collective-permute-start(bf16[512,512]{0,1:T(8,128)(2,1)S(1)} %fusion.54), channel_id=1, source_target_pairs={{0,8},{4,12},{8,16},{12,20},{16,24},{20,28},{1,9},{5,13},{9,17},{1... | collective-permute-start | bytes 1572872 | tf_op jit(solution)/shard_map/ppermute | solution.py:15
  213.4 25.8 %collective-permute-start.1 = (bf16[512,512]{0,1:T(8,128)(2,1)S(1)}, bf16[512,512]{0,1:T(8,128)(2,1)S(1)}, u32[]{:S(2)}, u32[]{:S(2)}) collective-permute-start(bf16[512,512]{0,1:T(8,128)(2,1)S(1)} %fusion.54), channel_id=1, source_target_pairs={{0,4},{4,8},{8,12},{12,16},{16,20},{20,24},{24,28},{1,5},{5,9},{9,... | collective-permute-start | bytes 1572872 | tf_op jit(solution)/shard_map/ppermute | solution.py:15
  239.1 0.6 copy-start.18
  276.8 4.6 copy-start
  283.1 33.2 %collective-permute-start.7 = (f32[512,512]{0,1:T(8,128)}, f32[512,512]{0,1:T(8,128)}, u32[]{:S(2)}, u32[]{:S(2)}) collective-permute-start(f32[512,512]{0,1:T(8,128)} %bitcast.23), channel_id=1, source_target_pairs={{4,0},{8,4},{12,8},{16,12},{20,16},{24,20},{28,24},{5,1},{9,5},{13... | collective-permute-start | bytes 3145736 | tf_op jit(solution)/shard_map/ppermute | solution.py:15
  284.4 56.2 %collective-permute-start.8 = (f32[512,512]{0,1:T(8,128)}, f32[512,512]{0,1:T(8,128)}, u32[]{:S(2)}, u32[]{:S(2)}) collective-permute-start(f32[512,512]{0,1:T(8,128)} %bitcast.24), channel_id=1, source_target_pairs={{8,0},{12,4},{16,8},{20,12},{24,16},{28,20},{9,1},{13,5},{17,9},{2... | collective-permute-start | bytes 3145736 | tf_op jit(solution)/shard_map/ppermute | solution.py:15
  300.8 51.8 %collective-permute-start.10 = (f32[512,512]{1,0:T(8,128)}, f32[512,512]{1,0:T(8,128)}, u32[]{:S(2)}, u32[]{:S(2)}) collective-permute-start(f32[512,512]{1,0:T(8,128)} %copy.73), channel_id=1, source_target_pairs={{8,0},{12,4},{16,8},{20,12},{24,16},{28,20},{9,1},{13,5},{17,9},{2... | collective-permute-start | bytes 3145736 | tf_op jit(solution)/shard_map/ppermute | solution.py:15
  303.4 49.2 %collective-permute-start.9 = (f32[512,512]{1,0:T(8,128)}, f32[512,512]{1,0:T(8,128)}, u32[]{:S(2)}, u32[]{:S(2)}) collective-permute-start(f32[512,512]{1,0:T(8,128)} %copy.71), channel_id=1, source_target_pairs={{4,0},{8,4},{12,8},{16,12},{20,16},{24,20},{28,24},{5,1},{9,5},{13... | collective-permute-start | bytes 3145736 | tf_op jit(solution)/shard_map/ppermute | solution.py:15
  313.7 1.1 copy-start.4
  316.3 27.3 %copy-start.5 = (f32[512,8,64]{0,2,1:T(8,128)S(1)}, f32[512,8,64]{0,2,1:T(8,128)}, u32[]{:S(2)}) copy-start(f32[512,8,64]{0,2,1:T(8,128)} %copy-done.4) | copy-start | bytes 3145732
  316.3 28.9 %copy-start.15 = (bf16[512,8,32]{0,2,1:T(8,128)(2,1)S(1)}, bf16[512,8,32]{0,2,1:T(8,128)(2,1)}, u32[]{:S(2)}) copy-start(bf16[512,8,32]{0,2,1:T(8,128)(2,1)} %slice.201) | copy-start | bytes 786436
  354.4 0.8 copy-start.7
  357.5 40.4 %copy-start.24 = (f32[8,1,256]{2,1,0:T(1,128)S(1)}, f32[8,1,256]{2,1,0:T(1,128)}, u32[]{:S(2)}) copy-start(f32[8,1,256]{2,1,0:T(1,128)} %convert_element_type.155) | copy-start | bytes 24580
  357.5 156.8 %reduce-scatter.12.cloned.1.call-start = ((), (), s32[]{:S(2)}) async-start(), calls=%async_computation.13 | async-start | bytes 5242880 | tf_op jit(solution)/shard_map/reduce_scatter | solution.py:274
  398.0 12.3 %copy-start.33 = (bf16[2048,2048]{1,0:T(8,128)(2,1)S(1)}, bf16[2048,2048]{1,0:T(8,128)(2,1)}, u32[]{:S(2)}) copy-start(bf16[2048,2048]{1,0:T(8,128)(2,1)} %all-gather.14.cloned.1.call-done) | copy-start | bytes 25165828
  410.2 4.8 copy-start.38
  410.2 4.8 copy-start.8
  410.2 4.8 copy-start.9
  410.3 4.8 copy-start.11
  422.9 0.7 copy-start.19
  423.0 170.9 %reduce-scatter.10.cloned.1.call-start = ((), (), s32[]{:S(2)}) async-start(), calls=%async_computation.12 | async-start | bytes 5242880 | tf_op jit(solution)/shard_map/reduce_scatter | solution.py:189
  423.7 11.6 %copy-start.39 = (f32[512,2048]{1,0:T(8,128)S(1)}, f32[512,2048]{1,0:T(8,128)}, u32[]{:S(2)}) copy-start(f32[512,2048]{1,0:T(8,128)} %fusion.76) | copy-start | bytes 12582916
  435.3 8.1 copy-start.13
  446.8 1.0 copy-start.10
  446.8 1.2 copy-start.12
  446.8 244.5 %reduce-scatter.14.cloned.1.call-start = ((), (), s32[]{:S(2)}) async-start(), calls=%async_computation.14 | async-start | bytes 14155776 | tf_op jit(solution)/shard_map/reduce_scatter | solution.py:279
  455.9 290.9 %reduce-scatter.16.cloned.1.call-start = ((), (), s32[]{:S(2)}) async-start(), calls=%async_computation.15 | async-start | bytes 4718592 | tf_op jit(solution)/shard_map/reduce_scatter | solution.py:281
  460.9 406.1 %reduce-scatter.20.cloned.1.call-start = ((), (), s32[]{:S(2)}) async-start(), calls=%async_computation.17 | async-start | bytes 18874368 | tf_op jit(solution)/shard_map/reduce_scatter | solution.py:284
  475.2 1.6 copy-start.34
  475.2 511.8 %reduce-scatter.18.cloned.1.call-start = ((), (), s32[]{:S(2)}) async-start(), calls=%async_computation.16 | async-start | bytes 18874368 | tf_op jit(solution)/shard_map/reduce_scatter | solution.py:282
  486.6 0.7 copy-start.36
  486.6 1.9 copy-start.27
  486.6 1.9 copy-start.28
  486.6 27.7 %copy-start.1 = (bf16[128,2048]{1,0:T(8,128)(2,1)S(1)}, bf16[128,2048]{1,0:T(8,128)(2,1)}, u32[]{:S(2)}) copy-start(bf16[128,2048]{1,0:T(8,128)(2,1)} %param.15) | copy-start | bytes 1572868
  486.6 27.7 %copy-start.17 = (f32[2048]{0:T(1024)S(1)}, f32[2048]{0:T(1024)}, u32[]{:S(2)}) copy-start(f32[2048]{0:T(1024)} %copy-done.16) | copy-start | bytes 24580
  486.6 27.7 %copy-start.23 = (f32[128]{0:T(128)S(1)}, f32[128]{0:T(128)}, u32[]{:S(2)}) copy-start(f32[128]{0:T(128)} %copy-done.22) | copy-start | bytes 1540
  486.6 29.3 %copy-start.32 = (f32[128]{0:T(128)S(1)}, f32[128]{0:T(128)}, u32[]{:S(2)}) copy-start(f32[128]{0:T(128)} %copy-done.31) | copy-start | bytes 1540
  486.6 29.3 %copy-start.26 = (f32[128]{0:T(128)S(1)}, f32[128]{0:T(128)}, u32[]{:S(2)}) copy-start(f32[128]{0:T(128)} %copy-done.25) | copy-start | bytes 1540
  486.6 107.2 %copy-start.3 = (bf16[128,2048]{1,0:T(8,128)(2,1)S(1)}, bf16[128,2048]{1,0:T(8,128)(2,1)}, u32[]{:S(2)}) copy-start(bf16[128,2048]{1,0:T(8,128)(2,1)} %param.26) | copy-start | bytes 1572868
  638.4 349.2 %copy-start.37 = (f32[64]{0:T(128)}, f32[64]{0:T(128)S(1)}, u32[]{:S(2)}) copy-start(f32[64]{0:T(128)S(1)} %dynamic-slice.2) | copy-start | bytes 772
Sparse Core Ops, SparseCore 0:
  58.0 64.5 all-gather.7
  125.0 45.3 all-gather.9
  172.3 33.7 all-gather.11
  207.9 64.8 all-gather.13
  274.6 123.3 all-gather.15
  401.4 33.6 reduce-scatter.21
  437.5 76.7 reduce-scatter.11
  516.6 77.2 reduce-scatter.9
  597.8 93.5 reduce-scatter.13
  695.5 51.3 reduce-scatter.15
  751.0 115.9 reduce-scatter.19
  871.0 115.9 reduce-scatter.17
